TPU v7x, 128 devices: a whole 4x4x4 slice. The times are simulated.
128 devices in a mesh: dp: 4 (over y), seq: 32 (over z, x, core).
Axes of the slice: x: 4, y: 4, z: 4, core: 2. Of those that a mesh axis runs over, the one named last changes fastest.
Arguments:
- queries: bfloat16 [4, 32768, 2048], P('dp', 'seq'), may hold values from -420 to 420
- keys: bfloat16 [4, 32768, 2048], P('dp', 'seq'), may hold values from -24 to 24
- values: bfloat16 [4, 32768, 2048], P('dp', 'seq'), may hold values from -12 to 12
- codes: int32 [4, 16, 32768], P('dp', None, 'seq'), may hold values from 0 to 511
- starts: int32 [4, 64], P('dp', 'seq'), may hold values from 0 to 1
- old_centroids: float32 [16, 512, 128], replicated, may hold values from -6 to 6
- old_counts: float32 [16, 512], replicated, may hold values from 4 to 64
Outputs:
- mixed: bfloat16 [4, 32768, 2048], P('dp', 'seq')
- codebook: float32 [16, 512, 128], P(None, 'dp')
All inputs are finite; a program needn't handle non-finite values.
Results may differ from a plain program's by a relative error of at most 0.0034.
Values sent between devices are 32-bit elements; how exact they have to be, the bound alone decides.
A program may use at most 384 MiB of HBM per device.

v0:
```python
import jax
import jax.numpy as jnp
from jax import lax
from jax.sharding import PartitionSpec as P

HEADS = 16
HEAD_DIM = 128
CODES = 512
BLOCK = 512
TOK_DEV = 1024
RETAIN = 0.9
NEGATIVE = -1e30


def prefix(part, axis, combine, identity):
    place = lax.axis_index(axis)
    gathered = jax.tree.map(lambda a: lax.all_gather(a, axis), part)
    state = jax.tree.map(lambda a, e: jnp.zeros_like(a) + jnp.asarray(e, a.dtype), part, identity)

    def one(hop, state):
        return combine(
            state, jax.tree.map(lambda a: lax.dynamic_index_in_dim(a, hop, 0, False), gathered)
        )

    return lax.fori_loop(0, place, one, state)


def one_hot_rows(code_block):
    return (code_block[:, :, None] == lax.iota(jnp.int32, CODES)[None, None, :]).astype(
        jnp.bfloat16
    )


def refresh_codes(sums, counts, centroids, previous):
    return (RETAIN * previous[..., None] * centroids + (1.0 - RETAIN) * sums) / (
        RETAIN * previous + (1.0 - RETAIN) * counts
    )[..., None]


def join_segments(earlier, later):
    survive = 1.0 - later[2][0]
    return (
        later[0] + survive * earlier[0],
        later[1] + survive * earlier[1],
        jnp.maximum(earlier[2], later[2]),
    )


def shards(queries, keys, values, codes, starts, old_centroids, old_counts):
    blocks_here = TOK_DEV // BLOCK
    flags = starts[0].astype(jnp.float32)
    key_sums = jnp.zeros((HEADS, CODES, HEAD_DIM), jnp.float32)
    code_counts = jnp.zeros((HEADS, CODES), jnp.float32)
    hot_list = []
    value_sums = []
    value_counts = []
    for block_id in range(blocks_here):
        offset = block_id * BLOCK
        hot_table = one_hot_rows(codes[0, :, offset : offset + BLOCK])
        key_part = keys[0, offset : offset + BLOCK].reshape(BLOCK, HEADS, HEAD_DIM)
        value_part = values[0, offset : offset + BLOCK].reshape(BLOCK, HEADS, HEAD_DIM)
        key_sums = key_sums + jnp.einsum(
            "hts,thd->hsd", hot_table, key_part, preferred_element_type=jnp.float32
        )
        counted = jnp.sum(hot_table, axis=1, dtype=jnp.float32)
        code_counts = code_counts + counted
        value_sums.append(
            jnp.einsum("hts,thd->hsd", hot_table, value_part, preferred_element_type=jnp.float32)
        )
        value_counts.append(counted)
        hot_list.append(hot_table)
    total_keys, total_counts = lax.psum((key_sums, code_counts), ("dp", "seq"))
    codebook = refresh_codes(total_keys, total_counts, old_centroids, old_counts)
    code_share = CODES // lax.axis_size("dp")
    codebook_out = lax.dynamic_slice_in_dim(
        codebook, lax.axis_index("dp") * code_share, code_share, 1
    )
    tail_sums = jnp.zeros((HEADS, CODES, HEAD_DIM), jnp.float32)
    tail_counts = jnp.zeros((HEADS, CODES), jnp.float32)
    flag_any = jnp.zeros((1,), jnp.float32)
    for block_id in range(blocks_here):
        survive = 1.0 - flags[block_id]
        tail_sums = survive * tail_sums + value_sums[block_id]
        tail_counts = survive * tail_counts + value_counts[block_id]
        flag_any = jnp.maximum(flag_any, flags[block_id])
    identity = (
        jnp.zeros_like(tail_sums),
        jnp.zeros_like(tail_counts),
        jnp.zeros((1,), jnp.float32),
    )
    enter_sums, enter_counts, ignored_flag = prefix(
        (tail_sums, tail_counts, flag_any), "seq", join_segments, identity
    )
    codebook_half = codebook.astype(jnp.bfloat16)
    score_scale = HEAD_DIM ** (-0.5)
    positions = lax.iota(jnp.int32, BLOCK)
    causal = positions[:, None] >= positions[None, :]
    run_sums = enter_sums
    run_counts = enter_counts
    outputs = []
    for block_id in range(blocks_here):
        offset = block_id * BLOCK
        survive = 1.0 - flags[block_id]
        cache_sums = survive * run_sums
        cache_counts = survive * run_counts
        code_means = (cache_sums / jnp.maximum(cache_counts, 1.0)[..., None]).astype(jnp.bfloat16)
        count_bias = jnp.where(cache_counts > 0, jnp.log(jnp.maximum(cache_counts, 1.0)), NEGATIVE)
        query_part = queries[0, offset : offset + BLOCK].reshape(BLOCK, HEADS, HEAD_DIM)
        value_part = values[0, offset : offset + BLOCK].reshape(BLOCK, HEADS, HEAD_DIM)
        code_scores = (
            jnp.einsum(
                "thd,hsd->hts", query_part, codebook_half, preferred_element_type=jnp.float32
            )
            * score_scale
            + count_bias[:, None, :]
        )
        key_codes = jnp.einsum(
            "hts,hsd->htd", hot_list[block_id], codebook_half, preferred_element_type=jnp.float32
        ).astype(jnp.bfloat16)
        local_scores = jnp.where(
            causal[None],
            jnp.einsum("ihd,hjd->hij", query_part, key_codes, preferred_element_type=jnp.float32)
            * score_scale,
            NEGATIVE,
        )
        row_top = jnp.maximum(jnp.max(code_scores, axis=-1), jnp.max(local_scores, axis=-1))
        code_weights = jnp.exp(code_scores - row_top[..., None])
        local_weights = jnp.where(causal[None], jnp.exp(local_scores - row_top[..., None]), 0.0)
        denominator = jnp.sum(code_weights, axis=-1) + jnp.sum(local_weights, axis=-1)
        mixed_part = jnp.einsum(
            "hts,hsd->htd",
            code_weights.astype(jnp.bfloat16),
            code_means,
            preferred_element_type=jnp.float32,
        )
        mixed_part = mixed_part + jnp.einsum(
            "hij,jhd->hid",
            local_weights.astype(jnp.bfloat16),
            value_part,
            preferred_element_type=jnp.float32,
        )
        out_rows = (
            (mixed_part / denominator[..., None])
            .transpose(1, 0, 2)
            .reshape(BLOCK, HEADS * HEAD_DIM)
            .astype(jnp.bfloat16)
        )
        outputs.append(out_rows)
        run_sums = cache_sums + value_sums[block_id]
        run_counts = cache_counts + value_counts[block_id]
    mixed = jnp.concatenate(outputs, axis=0)[None]
    return (mixed, codebook_out)


def solution(mesh):
    placed = (
        P("dp", "seq", None),
        P("dp", "seq", None),
        P("dp", "seq", None),
        P("dp", None, "seq"),
        P("dp", "seq"),
        P(),
        P(),
    )
    return jax.shard_map(
        shards,
        mesh=mesh,
        in_specs=placed,
        out_specs=(P("dp", "seq", None), P(None, "dp", None)),
        check_vma=False,
    )
```

profile of v0, /device:TPU:103, one launch (start us, length us, event | category | flops | bytes accessed | tf_op | source)
XLA Modules:
  0.0 883.3 jit_solution(4098301958992712305)
XLA Ops:
  8.8 4.0 fusion.78
  12.8 3.9 copy.85
  16.8 2.5 copy.86
  19.2 5.8 fusion.8
  25.0 5.7 fusion.61
  33.3 4.7 convert_reduce_fusion
  38.6 4.0 fusion.77
  42.6 4.0 copy.88
  46.6 2.5 copy.89
  49.1 5.8 fusion.6
  55.0 1.9 copy-done.10
  56.9 5.7 multiply_add_fusion.2
  63.9 4.2 fusion.76
  68.1 4.0 copy.87
  72.1 2.5 copy.90
  75.9 63.2 %all-reduce = f32[32]{0:T(128)S(1)} all-reduce(f32[32]{0:T(128)S(1)} %bitcast_dynamic-update-slice_fusion), channel_id=1, replica_groups=mesh['dp'=4,'seq'=32] {'seq'}, use_global_device_ids=true, to_apply=%add | all-reduce | flops 32 | bytes 256
  139.1 67.3 %psum.15 = f32[16,512]{1,0:T(8,128)S(1)} all-reduce(f32[16,512]{1,0:T(8,128)S(1)} %get-tuple-element.93), channel_id=1, replica_groups=mesh['dp'=4,'seq'=32] {'dp','seq'}, use_global_device_ids=true, to_apply=%region_3.0 | all-reduce | flops 8192 | bytes 65536 | tf_op jit(solution)/shard_map/psum | solution.py:72
  206.6 285.1 %all-reduce.3.cloned.1.call-done = f32[16,512,128]{2,1,0:T(8,128)} async-done(((f32[16,512,128]{2,1,0:T(8,128)}), f32[16,512,128]{2,1,0:T(8,128)}) %all-reduce.3.cloned.1.call-update) | async-done | bytes 4194320 | tf_op jit(solution)/shard_map/psum | solution.py:72
  491.7 5.1 fusion.74
  497.9 10.2 %fusion.14 = (f32[16,512]{1,0:T(8,128)S(1)}, f32[16,512,512]{2,1,0:T(8,128)}) fusion(pred[512,512]{0,1:T(8,128)(4,1)S(1)} %iota_compare_fusion.12, bf16[512,16,128]{0,2,1:T(8,128)(2,1)} %bitcast.107, bf16[16,512,128]{2,1,0:T(8,128)(2,1)S(1)} %get-tuple-element.82, s32[16,512]{1,0:T(8,128)S(1)} %get-tuple-element.95), kind=kOutput, calls=%fused_computation.27 | convolution fusion | flops 2165301248 | bytes 21299200 | tf_op jit(solution)/shard_map/ihd,hjd->hij/dot_general | solution.py:122
  508.1 2.5 broadcast.60
  510.6 261.9 %while.14 = (s32[]{:T(128)}, f32[16,512,128]{2,1,0:T(8,128)}, f32[16,512]{1,0:T(8,128)S(1)}, s32[]{:T(128)}, f32[32,16,512,128]{3,2,1,0:T(8,128)}, /*index=5*/f3...) while((s32[]{:T(128)}, f32[16,512,128]{2,1,0:T(8,128)}, ...), condition=%wide.region_5.6_spmd, body=%wide.region_4.5_spmd.sunk | while | flops 2113542 | bytes 12681379 | solution.py:25
  511.1 6.6 bitcast_add_fusion.4
  519.6 6.6 bitcast_add_fusion.4
  528.0 6.6 bitcast_add_fusion.4
  536.5 6.6 bitcast_add_fusion.4
  544.9 6.6 bitcast_add_fusion.4
  553.4 6.6 bitcast_add_fusion.4
  561.8 6.6 bitcast_add_fusion.4
  570.3 6.6 bitcast_add_fusion.4
  578.7 6.6 bitcast_add_fusion.4
  587.2 6.6 bitcast_add_fusion.4
  595.6 6.6 bitcast_add_fusion.4
  604.1 6.6 bitcast_add_fusion.4
  612.5 6.6 bitcast_add_fusion.4
  621.0 6.6 bitcast_add_fusion.4
  629.4 6.6 bitcast_add_fusion.4
  637.9 6.6 bitcast_add_fusion.4
  646.3 6.6 bitcast_add_fusion.4
  654.8 6.6 bitcast_add_fusion.4
  663.2 6.6 bitcast_add_fusion.4
  671.7 6.6 bitcast_add_fusion.4
  680.1 6.6 bitcast_add_fusion.4
  688.5 6.6 bitcast_add_fusion.4
  697.0 6.6 bitcast_add_fusion.4
  705.4 6.6 bitcast_add_fusion.4
  713.9 6.6 bitcast_add_fusion.4
  722.3 6.6 bitcast_add_fusion.4
  730.8 6.6 bitcast_add_fusion.4
  739.2 6.6 bitcast_add_fusion.4
  747.7 6.6 bitcast_add_fusion.4
  756.1 6.6 bitcast_add_fusion.4
  764.6 6.6 bitcast_add_fusion.4
  772.5 8.2 bitcast_reduce_fusion.1
  780.7 22.1 %fusion.20 = (f32[16,512]{1,0:T(8,128)S(1)}, f32[16,512]{1,0:T(8,128)S(1)}, f32[16,512]{1,0:T(8,128)S(1)}, f32[16,512,512]{2,1,0:T(8,128)}) fusion(f32[16,512,512]{2,1,0:T(8,128)} %get-tuple-element.107, f32[16,512]{1,0:T(8,128)S(1)} %max.29, pred[512,512]{0,1:T(8,128)(4,1)S(1)} %iota_compare_fusion.12, f32[16,512]{1,0:T(8,128)S(1)} %get-tuple-element.97, ...), kind=kOutput, calls=%fused_computation.33 | convolution fusion | flops 2203033600 | bytes 54984704 | tf_op jit(solution)/shard_map/ihd,hjd->hij/dot_general | solution.py:122
  802.8 9.5 %fusion.26 = f32[16,512,128]{1,2,0:T(8,128)S(1)} fusion(f32[16,512,512]{2,1,0:T(8,128)} %get-tuple-element.105, f32[16,512]{1,0:T(8,128)S(1)} %max.29, f32[16,512]{1,0:T(8,128)S(1)} %get-tuple-element.97, f32[16,512,128]{2,1,0:T(8,128)} %get-tuple-element.62, f32[16,512]{1,0:T(8,128)S(1)} %get-tuple-element.96, f32[]{:T(128)} %bitcast.8), kind=kOutput, calls=%fused_computation.38 | convolution fusion | flops 1093664768 | bytes 25264132 | tf_op jit(solution)/shard_map/hts,hsd->htd/dot_general | solution.py:130
  812.4 9.3 %fusion.47 = bf16[512,16,128]{0,2,1:T(8,128)(2,1)} fusion(f32[16,512,128]{1,2,0:T(8,128)S(1)} %fusion.26, f32[512,16]{0,1:T(8,128)S(1)} %add_bitcast_fusion.1, bf16[512,16,128]{0,2,1:T(8,128)(2,1)S(1)} %bitcast.112, f32[16,512,512]{2,1,0:T(8,128)} %get-tuple-element.107, f32[16,512]{1,0:T(8,128)S(1)} %max.29, pred[512,512]{0,1:T(8,128)(4,1)S(1)} %iota_compare_fusion.12), kind=kOutput, calls=%fused_computation.59 | convolution fusion | flops 1097859072 | bytes 25493504 | tf_op jit(solution)/shard_map/hij,jhd->hid/dot_general | solution.py:136
  821.7 4.0 copy.65
  825.7 4.3 bitcast_reduce_fusion
  830.0 16.9 %fusion.22 = (f32[16,512]{1,0:T(8,128)S(1)}, f32[16,512]{1,0:T(8,128)S(1)}) fusion(f32[16,512,512]{2,1,0:T(8,128)} %get-tuple-element.108, f32[16,512]{1,0:T(8,128)S(1)} %max.31, pred[512,512]{0,1:T(8,128)(4,1)S(1)} %iota_compare_fusion.12, f32[16,512]{1,0:T(8,128)S(1)} %get-tuple-element.91, f32[16,512,512]{2,1,0:T(8,128)S(1)} %get-tuple-element.103), kind=kLoop, calls=%fused_computation.35 | loop fusion | flops 37732352 | bytes 33947648 | tf_op jit(solution)/shard_map/reduce_sum | solution.py:129
  846.9 10.3 %fusion.24 = f32[16,512,128]{1,2,0:T(8,128)} fusion(f32[16,512,512]{2,1,0:T(8,128)} %copy-done.1, f32[16,512]{1,0:T(8,128)S(1)} %max.31, f32[16,512]{1,0:T(8,128)S(1)} %get-tuple-element.91, f32[16,512,128]{2,1,0:T(8,128)S(1)} %copy-done.11, f32[16,512,128]{2,1,0:T(8,128)S(1)} %copy-done, f32[16,512]{1,0:T(8,128)S(1)} %get-tuple-element.90, f32[]{:T(128)} %bitcast.8, ...), kind=kOutput, calls=%fused_computation.37 | convolution fusion | flops 1095761920 | bytes 29458440 | tf_op jit(solution)/shard_map/hts,hsd->htd/dot_general | solution.py:130
  857.2 10.3 %fusion.46 = bf16[512,16,128]{0,2,1:T(8,128)(2,1)} fusion(f32[16,512,128]{1,2,0:T(8,128)} %fusion.24, f32[512,16]{0,1:T(8,128)S(1)} %add_bitcast_fusion, bf16[512,16,128]{0,2,1:T(8,128)(2,1)S(1)} %bitcast.110, f32[16,512,512]{2,1,0:T(8,128)} %get-tuple-element.108, f32[16,512]{1,0:T(8,128)S(1)} %max.31, pred[512,512]{0,1:T(8,128)(4,1)S(1)} %iota_compare_fusion.12), kind=kOutput, calls=%fused_computation.57 | convolution fusion | flops 1097859072 | bytes 25493504 | tf_op jit(solution)/shard_map/hij,jhd->hid/dot_general | solution.py:136
  867.6 4.1 copy.66
  871.7 4.2 maximum_bitcast_fusion
  (109 shorter events, 63.8 us)
Async XLA Ops:
  8.0 483.7 %all-reduce.3.cloned.1.call-start = ((), (), s32[]{:S(2)}) async-start(), calls=%async_computation | async-start | bytes 8388608 | tf_op jit(solution)/shard_map/psum | solution.py:72
  19.2 5.8 copy-start.6
  30.7 0.7 copy-start.8
  30.8 477.4 %all-gather.7.cloned.1.call-start = ((), (), s32[]{:S(2)}) async-start(), calls=%async_computation.2 | async-start | bytes 1081344 | tf_op jit(solution)/shard_map/all_gather | solution.py:17
  38.6 469.6 %all-gather.5.cloned.1.call-start = ((), (), s32[]{:S(2)}) async-start(), calls=%async_computation.1 | async-start | bytes 138412032 | tf_op jit(solution)/shard_map/all_gather | solution.py:17
  49.1 7.7 copy-start.3
  54.9 1.9 copy-start.10
  68.1 6.5 copy-start.9
  68.1 138.4 %copy-start.7 = (f32[16,512]{1,0:T(8,128)S(1)}, f32[16,512]{1,0:T(8,128)}, u32[]{:S(2)}) copy-start(f32[16,512]{1,0:T(8,128)} %param.15) | copy-start | bytes 98308
  802.8 9.6 %copy-start.5 = (bf16[1,512,2048]{1,2,0:T(8,128)(2,1)S(1)}, bf16[1,512,2048]{1,2,0:T(8,128)(2,1)}, u32[]{:S(2)}) copy-start(bf16[1,512,2048]{1,2,0:T(8,128)(2,1)} %copy.88) | copy-start | bytes 6291460
  830.0 16.9 %copy-start.1 = (f32[16,512,512]{2,1,0:T(8,128)}, f32[16,512,512]{2,1,0:T(8,128)S(1)}, u32[]{:S(2)}) copy-start(f32[16,512,512]{2,1,0:T(8,128)S(1)} %get-tuple-element.103) | copy-start | bytes 50331652
  830.0 16.9 %copy-start = (f32[16,512,128]{2,1,0:T(8,128)S(1)}, f32[16,512,128]{2,1,0:T(8,128)}, u32[]{:S(2)}) copy-start(f32[16,512,128]{2,1,0:T(8,128)} %get-tuple-element.62) | copy-start | bytes 12582916
  830.0 16.9 %copy-start.11 = (f32[16,512,128]{2,1,0:T(8,128)S(1)}, f32[16,512,128]{2,1,0:T(8,128)}, u32[]{:S(2)}) copy-start(f32[16,512,128]{2,1,0:T(8,128)} %copy-done.10) | copy-start | bytes 12582916
  846.9 10.3 %copy-start.4 = (bf16[1,512,2048]{1,2,0:T(8,128)(2,1)S(1)}, bf16[1,512,2048]{1,2,0:T(8,128)(2,1)}, u32[]{:S(2)}) copy-start(bf16[1,512,2048]{1,2,0:T(8,128)(2,1)} %copy.89) | copy-start | bytes 6291460
  867.6 4.1 copy-start.2
Sparse Core Ops, SparseCore 0:
  30.9 460.7 all-reduce.2
Sparse Core Ops, SparseCore 1:
  38.7 42.5 all-gather.6
  83.9 378.2 all-gather.4
where the time goes:
time: 887 us; the launch traced here: 883 us
  other arithmetic  293 us (33%)
  waiting for transfers between devices  285 us (32%)
  blocking collectives  131 us (15%)
  matrix products  107 us (12%)
  local copies, waits for them, and re-layouts  48.4 us (5%)
  between operations  18.3 us (2%)
    psum x1, waiting for transfers between devices, shards(): total_keys, total_counts = lax.psum((key_sums, code_counts), ('dp', 'seq'))  285 us
    add x31, other arithmetic, join_segments(): later[0] + survive * earlier[0]  203 us
    psum x1, blocking collectives, shards(): total_keys, total_counts = lax.psum((key_sums, code_counts), ('dp', 'seq'))  67.3 us
    unnamed x1, blocking collectives  63.2 us
    add x31, other arithmetic, join_segments(): later[1] + survive * earlier[1]  41.4 us
    dot_general x2, matrix products, shards(): jnp.einsum('ihd,hjd->hij', query_part, key_codes, preferred_element_type=...  32.3 us
    unnamed x33, local copies, waits for them, and re-layouts  23.2 us
    dot_general x2, matrix products, shards(): jnp.einsum('hts,hsd->htd', code_weights.astype(jnp.bfloat16), code_means,...  19.9 us
  transfers between devices with their start and end apart: 3, of which 1 were waited for; matrix products, arithmetic and copies ran while one was open for 6% of the time, Pallas kernels for 0%

commit v1 on v0

--- a/solution.py
+++ b/solution.py
@@ -2,6 +2,7 @@
 import jax.numpy as jnp
 from jax import lax
 from jax.sharding import PartitionSpec as P
+from jax.lax import psum
 
 HEADS = 16
 HEAD_DIM = 128
@@ -69,7 +70,7 @@
         )
         value_counts.append(counted)
         hot_list.append(hot_table)
-    total_keys, total_counts = lax.psum((key_sums, code_counts), ("dp", "seq"))
+    total_keys, total_counts = psum(psum((key_sums, code_counts), "dp"), "seq")
     codebook = refresh_codes(total_keys, total_counts, old_centroids, old_counts)
     code_share = CODES // lax.axis_size("dp")
     codebook_out = lax.dynamic_slice_in_dim(

time: 887 us -> 1040 us (1.17)
  waiting for transfers between devices: 285 us -> 433 us
    all_gather x2, waiting for transfers between devices: 0.01 us -> 339 us  [prefix(): gathered = jax.tree.map(lambda a: lax.all_gather(a, axis), part)]
    psum x1 -> x2, waiting for transfers between devices: 285 us -> 94.1 us  [shards(): total_keys, total_counts = psum(psum((key_sums, code_counts), 'dp'), 'seq')]
    psum x1 -> x2, blocking collectives: 67.3 us -> 135 us  [shards(): total_keys, total_counts = psum(psum((key_sums, code_counts), 'dp'), 'seq')]
    unnamed x1 -> x0, blocking collectives: 63.2 us -> none
  transfers between devices with their start and end apart: 3 -> 4, of which waited for: 1 -> 2; matrix products, arithmetic and copies ran while one was open for 6% -> 6% of each run, Pallas kernels for 0% -> 0%
where the time goes in v1:
time: 1040 us; the launch traced here: 1030 us
  waiting for transfers between devices  433 us (42%)
  other arithmetic  294 us (28%)
  blocking collectives  135 us (13%)
  matrix products  107 us (10%)
  local copies, waits for them, and re-layouts  47.9 us (5%)
  between operations  16.6 us (2%)
    all_gather x2, waiting for transfers between devices, prefix(): gathered = jax.tree.map(lambda a: lax.all_gather(a, axis), part)  339 us
    add x31, other arithmetic, join_segments(): later[0] + survive * earlier[0]  203 us
    psum x2, blocking collectives, shards(): total_keys, total_counts = psum(psum((key_sums, code_counts), 'dp'), 'seq')  135 us
    psum x2, waiting for transfers between devices, shards(): total_keys, total_counts = psum(psum((key_sums, code_counts), 'dp'), 'seq')  94.1 us
    add x31, other arithmetic, join_segments(): later[1] + survive * earlier[1]  41.4 us
    dot_general x2, matrix products, shards(): jnp.einsum('ihd,hjd->hij', query_part, key_codes, preferred_element_type=...  32.3 us
    unnamed x33, local copies, waits for them, and re-layouts  22.8 us
  transfers between devices with their start and end apart: 4, of which 2 were waited for; matrix products, arithmetic and copies ran while one was open for 6% of the time, Pallas kernels for 0%

profile of v1, /device:TPU:103, one launch (start us, length us, event | category | flops | bytes accessed | tf_op | source)
XLA Modules:
  0.0 1034.8 jit_solution(2718840360308776661)
XLA Ops:
  8.0 4.0 fusion.78
  12.0 3.9 copy.85
  15.9 2.5 copy.86
  18.4 5.8 fusion.8
  24.2 5.7 fusion.61
  30.0 94.1 %all-reduce.5.cloned.1.call-done = f32[16,512,128]{2,1,0:T(8,128)} async-done(((f32[16,512,128]{2,1,0:T(8,128)}), f32[16,512,128]{2,1,0:T(8,128)}) %all-reduce.5.cloned.1.call-update) | async-done | bytes 4194320 | tf_op jit(solution)/shard_map/psum | solution.py:73
  126.0 4.7 convert_reduce_fusion
  131.4 4.0 fusion.77
  135.4 4.2 copy.88
  139.6 2.5 copy.89
  142.1 5.8 fusion.6
  149.8 5.7 multiply_add_fusion.2
  156.9 4.1 fusion.76
  161.0 4.0 copy.87
  165.0 2.5 copy.90
  168.8 11.6 %psum.30 = f32[16,512]{1,0:T(8,128)S(1)} all-reduce(f32[16,512]{1,0:T(8,128)S(1)} %get-tuple-element.95), channel_id=1, replica_groups=mesh['dp'=4,'seq'=32] {'dp'}, use_global_device_ids=true, to_apply=%region_4.0 | all-reduce | flops 8192 | bytes 65536 | tf_op jit(solution)/shard_map/psum | solution.py:73
  180.4 123.7 %all-reduce.1 = (f32[16,512]{1,0:T(8,128)S(1)}, f32[32]{0:T(128)S(1)}) all-reduce(f32[16,512]{1,0:T(8,128)S(1)} %psum.30, f32[32]{0:T(128)S(1)} %bitcast_dynamic-update-slice_fusion), channel_id=1, replica_groups=mesh['dp'=4,'seq'=32] {'seq'}, use_global_device_ids=true, to_apply=%region_5.0 | all-reduce | flops 8224 | bytes 65792 | tf_op jit(solution)/shard_map/psum | solution.py:73
  304.3 5.8 fusion.74
  311.1 10.3 fusion.14
  321.4 339.3 %all-gather.5.cloned.1.call-done = f32[512,512,128]{2,1,0:T(8,128)} async-done(((f32[16,512,128]{2,1,0:T(8,128)}), f32[512,512,128]{2,1,0:T(8,128)}) %all-gather.5.cloned.1.call-update) | async-done | bytes 134217744 | tf_op jit(solution)/shard_map/all_gather | solution.py:18
  660.7 2.5 broadcast.60
  663.1 261.9 %while.14 = (s32[]{:T(128)}, f32[16,512,128]{2,1,0:T(8,128)}, f32[16,512]{1,0:T(8,128)S(1)}, s32[]{:T(128)}, f32[32,16,512,128]{3,2,1,0:T(8,128)}, /*index=5*/f3...) while((s32[]{:T(128)}, f32[16,512,128]{2,1,0:T(8,128)}, ...), condition=%wide.region_7.8_spmd, body=%wide.region_6.7_spmd.sunk | while | flops 2113542 | bytes 12681379 | solution.py:26
  663.7 6.6 bitcast_add_fusion.4
  672.1 6.6 bitcast_add_fusion.4
  680.6 6.6 bitcast_add_fusion.4
  689.0 6.6 bitcast_add_fusion.4
  697.5 6.6 bitcast_add_fusion.4
  705.9 6.6 bitcast_add_fusion.4
  714.3 6.6 bitcast_add_fusion.4
  722.8 6.6 bitcast_add_fusion.4
  731.2 6.6 bitcast_add_fusion.4
  739.7 6.6 bitcast_add_fusion.4
  748.1 6.6 bitcast_add_fusion.4
  756.6 6.6 bitcast_add_fusion.4
  765.0 6.6 bitcast_add_fusion.4
  773.5 6.6 bitcast_add_fusion.4
  781.9 6.6 bitcast_add_fusion.4
  790.4 6.6 bitcast_add_fusion.4
  798.8 6.6 bitcast_add_fusion.4
  807.3 6.6 bitcast_add_fusion.4
  815.7 6.6 bitcast_add_fusion.4
  824.2 6.6 bitcast_add_fusion.4
  832.6 6.6 bitcast_add_fusion.4
  841.1 6.6 bitcast_add_fusion.4
  849.5 6.6 bitcast_add_fusion.4
  858.0 6.6 bitcast_add_fusion.4
  866.4 6.6 bitcast_add_fusion.4
  874.9 6.6 bitcast_add_fusion.4
  883.3 6.6 bitcast_add_fusion.4
  891.8 6.6 bitcast_add_fusion.4
  900.2 6.6 bitcast_add_fusion.4
  908.6 6.6 bitcast_add_fusion.4
  917.1 6.6 bitcast_add_fusion.4
  925.0 8.2 bitcast_reduce_fusion.1
  933.3 22.1 %fusion.20 = (f32[16,512]{1,0:T(8,128)S(1)}, f32[16,512]{1,0:T(8,128)S(1)}, f32[16,512]{1,0:T(8,128)S(1)}, f32[16,512,512]{2,1,0:T(8,128)}) fusion(f32[16,512,512]{2,1,0:T(8,128)} %get-tuple-element.109, f32[16,512]{1,0:T(8,128)S(1)} %max.29, pred[512,512]{0,1:T(8,128)(4,1)S(1)} %iota_compare_fusion.12, f32[16,512]{1,0:T(8,128)S(1)} %get-tuple-element.99, ...), kind=kOutput, calls=%fused_computation.33 | convolution fusion | flops 2203033600 | bytes 54984704 | tf_op jit(solution)/shard_map/ihd,hjd->hij/dot_general | solution.py:123
  955.3 9.5 fusion.26
  964.9 9.3 fusion.47
  974.2 4.0 copy.65
  978.2 4.3 bitcast_reduce_fusion
  982.5 16.7 %fusion.22 = (f32[16,512]{1,0:T(8,128)S(1)}, f32[16,512]{1,0:T(8,128)S(1)}) fusion(f32[16,512,512]{2,1,0:T(8,128)} %get-tuple-element.110, f32[16,512]{1,0:T(8,128)S(1)} %max.31, pred[512,512]{0,1:T(8,128)(4,1)S(1)} %iota_compare_fusion.12, f32[16,512]{1,0:T(8,128)S(1)} %get-tuple-element.93, f32[16,512,512]{2,1,0:T(8,128)S(1)} %get-tuple-element.105), kind=kLoop, calls=%fused_computation.35 | loop fusion | flops 37732352 | bytes 33947648 | tf_op jit(solution)/shard_map/reduce_sum | solution.py:130
  999.3 10.3 fusion.24
  1009.6 10.3 fusion.46
  1019.9 4.1 copy.66
  1024.1 4.2 maximum_bitcast_fusion
  (112 shorter events, 65.2 us)
Async XLA Ops:
  7.2 116.9 %all-reduce.5.cloned.1.call-start = ((), (), s32[]{:S(2)}) async-start(), calls=%async_computation | async-start | bytes 8388608 | tf_op jit(solution)/shard_map/psum | solution.py:73
  18.4 5.8 copy-start.6
  29.9 94.3 %copy-start.8 = (s32[1,2]{1,0:T(1,128)S(1)}, s32[1,2]{1,0:T(1,128)}, u32[]{:S(2)}) copy-start(s32[1,2]{1,0:T(1,128)} %param.13) | copy-start | bytes 28
  29.9 274.4 %all-reduce.7.cloned.1.call-start = ((), (), s32[]{:S(2)}) async-start(), calls=%async_computation.1 | async-start | bytes 8388608 | tf_op jit(solution)/shard_map/psum | solution.py:73
  124.1 197.3 %all-gather.7.cloned.1.call-start = ((), (), s32[]{:S(2)}) async-start(), calls=%async_computation.3 | async-start | bytes 1081344 | tf_op jit(solution)/shard_map/all_gather | solution.py:18
  131.4 529.3 %all-gather.5.cloned.1.call-start = ((), (), s32[]{:S(2)}) async-start(), calls=%async_computation.2 | async-start | bytes 138412032 | tf_op jit(solution)/shard_map/all_gather | solution.py:18
  142.1 7.7 copy-start.3
  147.9 1.9 copy-start.10
  161.0 6.5 copy-start.9
  161.0 143.2 %copy-start.7 = (f32[16,512]{1,0:T(8,128)S(1)}, f32[16,512]{1,0:T(8,128)}, u32[]{:S(2)}) copy-start(f32[16,512]{1,0:T(8,128)} %param.15) | copy-start | bytes 98308
  955.3 9.6 copy-start.5
  982.5 16.8 %copy-start.1 = (f32[16,512,512]{2,1,0:T(8,128)}, f32[16,512,512]{2,1,0:T(8,128)S(1)}, u32[]{:S(2)}) copy-start(f32[16,512,512]{2,1,0:T(8,128)S(1)} %get-tuple-element.105) | copy-start | bytes 50331652
  982.5 16.7 %copy-start = (f32[16,512,128]{2,1,0:T(8,128)S(1)}, f32[16,512,128]{2,1,0:T(8,128)}, u32[]{:S(2)}) copy-start(f32[16,512,128]{2,1,0:T(8,128)} %get-tuple-element.62) | copy-start | bytes 12582916
  982.5 16.7 %copy-start.11 = (f32[16,512,128]{2,1,0:T(8,128)S(1)}, f32[16,512,128]{2,1,0:T(8,128)}, u32[]{:S(2)}) copy-start(f32[16,512,128]{2,1,0:T(8,128)} %copy-done.10) | copy-start | bytes 12582916
  999.3 10.3 copy-start.4
  1019.9 4.1 copy-start.2
Sparse Core Ops, SparseCore 0:
  30.0 94.0 all-reduce.4
  127.8 110.5 all-reduce.6
  241.0 41.5 all-gather.6
  285.5 375.1 all-gather.4
